TPU v7x, 32 devices: a whole 2x2x4 slice. The times are simulated.
32 devices in a mesh: grp: 2 (over y), pol: 16 (over z, x, core).
Axes of the slice: x: 2, y: 2, z: 4, core: 2. Of those that a mesh axis runs over, the one named last changes fastest.
Arguments:
- shocks: float32 [6, 128, 1024], P('grp'), parts along dimension 0, may hold values from -6 to 6
- loadings: float32 [1024, 128], P('pol'), may hold values from -0.5 to 0.5
- sec_drift: float32 [1024], P('pol'), may hold values from -0.02 to 0.08
- holdings: float32 [1024, 128], P('pol'), may hold values from -0.1875 to 0.1875
- fund_of: int32 [8192, 1], P('pol'), may hold values from 0 to 127
- product_type: int32 [8192], P('pol'), may hold values from 0 to 7
- term_years: int32 [8192], P('pol'), may hold values from 1 to 3
- asset_start: float32 [8192], P('pol'), may hold values from 0.35 to 3
- liab_start: float32 [8192], P('pol'), may hold values from 0.3 to 3
- base_lapse: float32 [8], replicated, may hold values from 0.02 to 0.2
- guarantee: float32 [8], replicated, may hold values from 0 to 0.08
- lapse_draw: bfloat16 [8192, 6, 1024], P('pol', 'grp'), parts along dimension 1, may hold values from 0 to 1
Outputs:
- assets: float32 [8192, 2048], P('pol', 'grp'), parts along dimension 1
- liability: float32 [8192, 2048], P('pol', 'grp'), parts along dimension 1
- credit_rates: float32 [6, 128, 1024], P('grp', None, 'pol'), parts along dimension 0
There are 2 independent parts, one for each index of `grp`. A program takes and returns all parts, laid end to end along the dimension named above; an argument that names none is the same for every part. Nothing has to cross between parts.
Inputs may be any that keep to these rules, and one draw needn't show every extreme that they name: `fund_of`: every fund backs at least one policy.
All inputs are finite; a program needn't handle non-finite values.
Results may differ from a plain program's by a relative error of at most 0.0003.
Values sent between devices are 32-bit elements; how exact they have to be, the bound alone decides.
A program may use at most 64 MiB of HBM per device.

v0:
```python
import jax
import jax.numpy as jnp
from jax import lax
from jax.sharding import PartitionSpec as P


def crediting(totals):
    return 0.01 + jax.nn.softplus(20.0 * (totals[0] / totals[1] - 1.05)) / 20.0


def local(
    shocks,
    loadings,
    sec_drift,
    holdings,
    fund_of,
    product_type,
    term_years,
    asset_start,
    liab_start,
    base_lapse,
    guarantee,
    lapse_draw,
):
    highest = lax.Precision.HIGHEST
    num_years = shocks.shape[0]
    num_paths = shocks.shape[2]
    num_funds = holdings.shape[1]
    sec_ret = (
        0.25 * jnp.tanh(jnp.einsum("sk,ykp->ysp", loadings, shocks, precision=highest))
        + sec_drift[None, :, None]
    )
    partial_funds = jnp.einsum("sf,ysp->yfp", holdings, sec_ret, precision=highest)
    fund_ret = lax.psum(partial_funds, "pol")
    member = (fund_of[:, 0][:, None] == jnp.arange(num_funds, dtype=jnp.int32)[None, :]).astype(
        jnp.float32
    )
    type_hot = (
        product_type[:, None] == jnp.arange(base_lapse.shape[0], dtype=jnp.int32)[None, :]
    ).astype(jnp.float32)
    guaranteed = jnp.sum(type_hot * guarantee[None, :], axis=1)
    base_rate = jnp.sum(type_hot * base_lapse[None, :], axis=1)
    count = asset_start.shape[0]
    assets = jnp.broadcast_to(asset_start[:, None], (count, num_paths))
    liability = jnp.broadcast_to(liab_start[:, None], (count, num_paths))
    owned_paths = num_paths // lax.axis_size("pol")
    first_path = lax.axis_index("pol") * owned_paths
    collected = []
    for year in range(num_years):
        year_ret = fund_ret[year]
        in_force = (term_years > year).astype(jnp.float32)[:, None]
        growth = jnp.dot(member, year_ret, precision=highest)
        assets = assets * (1.0 + in_force * growth)
        fund_sums = jnp.stack(
            [
                jnp.dot(member.T, in_force * assets, precision=highest),
                jnp.dot(member.T, liability, precision=highest),
            ]
        )
        totals = lax.psum(fund_sums, "pol")
        declared = crediting(totals)
        own_rates = lax.dynamic_slice_in_dim(declared, first_path, owned_paths, 1)
        collected.append(own_rates)
        credit = jnp.maximum(jnp.dot(member, declared, precision=highest), guaranteed[:, None])
        lapse_rate = jnp.minimum(
            base_rate[:, None]
            * (0.5 + lapse_draw[:, year, :].astype(jnp.float32))
            * jnp.exp(5.0 * (growth - credit)),
            0.5,
        )
        liability = liability * (1.0 + in_force * credit) * (1.0 - in_force * lapse_rate)
        assets = assets * (1.0 - in_force * lapse_rate)
    return (assets, liability, jnp.stack(collected))


def solution(mesh):
    in_specs = (
        P("grp", None, None),
        P("pol", None),
        P("pol"),
        P("pol", None),
        P("pol", None),
        P("pol"),
        P("pol"),
        P("pol"),
        P("pol"),
        P(),
        P(),
        P("pol", "grp", None),
    )
    out_specs = (P("pol", "grp"), P("pol", "grp"), P("grp", None, "pol"))
    return jax.shard_map(local, mesh=mesh, in_specs=in_specs, out_specs=out_specs, check_vma=False)
```

profile of v0, /device:TPU:0, one launch (start us, length us, event | category | flops | bytes accessed | tf_op | source)
XLA Modules:
  0.0 433.8 jit_solution(17481085283756002193)
XLA Ops:
  7.2 0.0 copy-start
  7.2 0.0 copy-start.12
  7.2 0.0 all-reduce.5.cloned.1.call-start
  7.2 1.3 copy-done
  8.6 1.8 fusion.20
  10.4 0.0 copy-done.12
  10.4 0.0 copy-start.11
  10.4 0.0 copy-start.17
  10.4 0.0 copy-start.14
  10.4 3.8 convolution_bitcast_fusion
  14.2 0.0 all-reduce.5.cloned.1.call-update
  14.2 0.0 all-reduce.7.cloned.1.call-start
  14.3 0.0 copy-done.11
  14.3 0.0 copy-done.17
  14.3 1.6 convolution_bitcast_fusion.3
  15.9 0.0 copy-done.14
  15.9 97.1 %all-reduce.5.cloned.1.call-done = f32[3,128,1024]{1,2,0:T(8,128)} async-done(((f32[3,128,1024]{1,2,0:T(8,128)}), f32[3,128,1024]{1,2,0:T(8,128)}) %all-reduce.5.cloned.1.call-update) | async-done | bytes 1572880 | tf_op jit(solution)/shard_map/psum | solution.py:34
  113.0 2.1 fusion.53
  115.1 0.0 copy-start.7
  115.1 0.0 copy-start.10
  115.1 1.3 copy-done.7
  116.4 1.3 fusion.27
  117.7 0.0 copy-start.13
  117.7 0.0 copy-start.15
  117.7 0.0 copy-start.16
  117.7 1.0 pad_maximum_fusion
  118.8 0.0 all-reduce.7.cloned.1.call-update
  118.8 0.0 all-reduce.9.cloned.1.call-start
  118.8 0.0 copy-done.13
  118.8 0.0 copy-done.15
  118.9 0.0 copy-done.16
  118.9 0.1 select_reduce_fusion.1
  119.0 0.6 copy-done.8
  119.5 2.3 fusion.49
  121.9 89.7 %all-reduce.7.cloned.1.call-done = f32[2,128,1024]{2,1,0:T(8,128)} async-done(((f32[2,128,1024]{2,1,0:T(8,128)}), f32[2,128,1024]{2,1,0:T(8,128)}) %all-reduce.7.cloned.1.call-update) | async-done | bytes 1048592 | tf_op jit(solution)/shard_map/psum | solution.py:60
  211.5 1.6 fusion.37
  213.1 4.7 %multiply_multiply_fusion.2 = (f32[512,1024]{1,0:T(8,128)S(1)}, f32[512,1024]{1,0:T(8,128)S(1)}) fusion(f32[512,1024]{1,0:T(8,128)} %copy-done.7, f32[512]{0:T(512)S(1)} %get-tuple-element.4, f32[512]{0:T(512)S(1)} %get-tuple-element.3, f32[512]{0:T(512)S(1)} %get-tuple-element.11, f32[512]{0:T(512)S(1)} %copy-done.17, bf16[512,3,1024]{2,0,1:T(8,128)(2,1)} %param.23, ...), kind=kOutput, calls=%fused_computation.20 | convolution fusion | flops 816381952 | bytes 9975808 | tf_op jit(solution)/shard_map/dot_general | solution.py:64
  217.9 0.0 copy-start.6
  217.9 1.1 fusion.21
  219.0 1.0 convolution_bitcast_fusion.2
  220.0 1.1 pad_maximum_fusion.1
  221.0 0.0 all-reduce.9.cloned.1.call-update
  221.1 0.2 all-reduce.11.cloned.1.call-start
  221.3 2.3 fusion.45
  223.6 90.4 %all-reduce.9.cloned.1.call-done = f32[2,128,1024]{2,1,0:T(8,128)} async-done(((f32[2,128,1024]{2,1,0:T(8,128)}), f32[2,128,1024]{2,1,0:T(8,128)}) %all-reduce.9.cloned.1.call-update) | async-done | bytes 1048592 | tf_op jit(solution)/shard_map/psum | solution.py:60
  314.1 1.6 fusion.39
  315.7 4.2 multiply_multiply_fusion.1
  319.9 0.0 copy-start.4
  319.9 0.0 copy-start.5
  319.9 1.0 convolution_bitcast_fusion.1
  320.9 0.0 copy-done.3
  320.9 2.1 copy-done.2
  323.0 1.3 fusion.24
  324.4 1.1 pad_maximum_fusion.2
  325.5 0.0 all-reduce.11.cloned.1.call-update
  325.5 0.9 constant_dynamic-slice_fusion.2
  326.4 0.1 copy.18
  326.5 92.0 %all-reduce.11.cloned.1.call-done = f32[2,128,1024]{2,1,0:T(8,128)} async-done(((f32[2,128,1024]{2,1,0:T(8,128)}), f32[2,128,1024]{2,1,0:T(8,128)}) %all-reduce.11.cloned.1.call-update) | async-done | bytes 1048592 | tf_op jit(solution)/shard_map/psum | solution.py:60
  418.4 1.6 fusion.41
  420.0 0.1 constant_dynamic-slice_fusion
  420.1 6.3 %multiply_multiply_fusion = (f32[512,1024]{1,0:T(8,128)}, f32[512,1024]{1,0:T(8,128)}) fusion(f32[512,1024]{1,0:T(8,128)} %copy-done.5, f32[512]{0:T(512)S(1)} %get-tuple-element.12, f32[512]{0:T(512)S(1)} %get-tuple-element.4, f32[512,1024]{1,0:T(8,128)} %fusion.45, bf16[512,3,1024]{2,0,1:T(8,128)(2,1)} %param.23, f32[512]{0:T(512)S(1)} %get-tuple-element.3, ...), kind=kOutput, calls=%fused_computation.15 | convolution fusion | flops 815333376 | bytes 14163968 | tf_op jit(solution)/shard_map/dot_general | solution.py:64
  426.5 0.1 copy.19
  426.5 0.1 copy.20
  426.6 0.7 pad_maximum_fusion.3
  (14 shorter events, 0.0 us)
Async XLA Ops:
  7.2 1.4 copy-start
  7.2 3.2 copy-start.12
  7.2 105.8 %all-reduce.5.cloned.1.call-start = ((), (), s32[]{:S(2)}) async-start(), calls=%async_computation | async-start | bytes 3145728 | tf_op jit(solution)/shard_map/psum | solution.py:34
  10.4 3.9 copy-start.11
  10.4 3.9 copy-start.17
  10.4 5.5 %copy-start.14 = (s32[512]{0:T(512)S(1)}, s32[512]{0:T(512)}, u32[]{:S(2)}) copy-start(s32[512]{0:T(512)} %param.18) | copy-start | bytes 6148
  14.2 102.2 %copy-start.18 = (f32[512]{0:T(512)S(1)}, f32[512]{0:T(512)}, u32[]{:S(2)}) copy-start(f32[512]{0:T(512)} %param.19) | copy-start | bytes 6148
  14.2 197.3 %all-reduce.7.cloned.1.call-start = ((), (), s32[]{:S(2)}) async-start(), calls=%async_computation.1 | async-start | bytes 2097152 | tf_op jit(solution)/shard_map/psum | solution.py:60
  115.1 1.3 copy-start.7
  115.1 2.6 copy-start.10
  117.7 1.2 copy-start.13
  117.7 1.2 copy-start.15
  117.7 1.1 copy-start.16
  117.7 1.8 copy-start.8
  118.8 195.3 %all-reduce.9.cloned.1.call-start = ((), (), s32[]{:S(2)}) async-start(), calls=%async_computation.2 | async-start | bytes 2097152 | tf_op jit(solution)/shard_map/psum | solution.py:60
  213.1 4.8 %copy-start.9 = (f32[128,1024]{1,0:T(8,128)}, f32[128,1024]{1,0:T(8,128)S(1)}, u32[]{:S(2)}) copy-start(f32[128,1024]{1,0:T(8,128)S(1)} %fusion.37) | copy-start | bytes 1572868
  217.9 2.1 copy-start.1
  217.9 2.1 copy-start.6
  221.1 197.4 %all-reduce.11.cloned.1.call-start = ((), (), s32[]{:S(2)}) async-start(), calls=%async_computation.3 | async-start | bytes 2097152 | tf_op jit(solution)/shard_map/psum | solution.py:60
  315.7 5.2 %copy-start.3 = (f32[512,1024]{1,0:T(8,128)S(1)}, f32[512,1024]{1,0:T(8,128)}, u32[]{:S(2)}) copy-start(f32[512,1024]{1,0:T(8,128)} %fusion.45) | copy-start | bytes 6291460
  319.9 4.5 %copy-start.4 = (f32[512,1024]{1,0:T(8,128)}, f32[512,1024]{1,0:T(8,128)S(1)}, u32[]{:S(2)}) copy-start(f32[512,1024]{1,0:T(8,128)S(1)} %get-tuple-element.6) | copy-start | bytes 6291460
  319.9 4.5 %copy-start.5 = (f32[512,1024]{1,0:T(8,128)}, f32[512,1024]{1,0:T(8,128)S(1)}, u32[]{:S(2)}) copy-start(f32[512,1024]{1,0:T(8,128)S(1)} %get-tuple-element.5) | copy-start | bytes 6291460
  319.9 3.1 copy-start.2
Sparse Core Ops, SparseCore 0:
  14.4 98.6 all-reduce.4
  118.9 92.5 all-reduce.6
  221.2 92.8 all-reduce.8
  325.6 92.7 all-reduce.10
where the time goes:
time: 434 us
  waiting for transfers between devices  369 us (85%)
  matrix products  34.8 us (8%)
  between operations  14.1 us (3%)
  other arithmetic  8.72 us (2%)
  local copies, waits for them, and re-layouts  6.66 us (2%)
    psum x3, waiting for transfers between devices, local(): totals = lax.psum(fund_sums, 'pol')  272 us
    psum x1, waiting for transfers between devices, local(): fund_ret = lax.psum(partial_funds, 'pol')  97.1 us
    dot_general x3, matrix products, local(): jnp.dot(member, declared, precision=highest)  15.3 us
  transfers between devices with their start and end apart: 4, of which 4 were waited for; matrix products, arithmetic and copies ran while one was open for 2% of the time, Pallas kernels for 0%

commit v1 on v0

--- a/solution.py
+++ b/solution.py
@@ -31,7 +31,7 @@
         + sec_drift[None, :, None]
     )
     partial_funds = jnp.einsum("sf,ysp->yfp", holdings, sec_ret, precision=highest)
-    fund_ret = lax.psum(partial_funds, "pol")
+    fund_ret = jnp.sum(lax.all_gather(partial_funds, "pol"), axis=0)
     member = (fund_of[:, 0][:, None] == jnp.arange(num_funds, dtype=jnp.int32)[None, :]).astype(
         jnp.float32
     )

time: 434 us -> 477 us (1.099)
  waiting for transfers between devices: 369 us -> 404 us
  other arithmetic: 8.72 us -> 18.1 us
    all_gather x0 -> x1, waiting for transfers between devices: none -> 130 us  [local(): fund_ret = jnp.sum(lax.all_gather(partial_funds, 'pol'), axis=0)]
    psum x1 -> x0, waiting for transfers between devices: 97.1 us -> none  [local(): fund_ret = lax.psum(partial_funds, 'pol')]
    reduce_sum x0 -> x1, other arithmetic: none -> 9.34 us  [local(): fund_ret = jnp.sum(lax.all_gather(partial_funds, 'pol'), axis=0)]
where the time goes in v1:
time: 477 us; the launch traced here: 476 us
  waiting for transfers between devices  404 us (85%)
  matrix products  32.6 us (7%)
  other arithmetic  18.1 us (4%)
  between operations  14.1 us (3%)
  local copies, waits for them, and re-layouts  7.71 us (2%)
    psum x3, waiting for transfers between devices, local(): totals = lax.psum(fund_sums, 'pol')  274 us
    all_gather x1, waiting for transfers between devices, local(): fund_ret = jnp.sum(lax.all_gather(partial_funds, 'pol'), axis=0)  130 us
    dot_general x3, matrix products, local(): jnp.dot(member, declared, precision=highest)  15.3 us
  transfers between devices with their start and end apart: 4, of which 4 were waited for; matrix products, arithmetic and copies ran while one was open for 2% of the time, Pallas kernels for 0%

profile of v1, /device:TPU:0, one launch (start us, length us, event | category | flops | bytes accessed | tf_op | source)
XLA Modules:
  0.0 476.4 jit_solution(7995390864021022172)
XLA Ops:
  7.2 0.0 copy-start
  7.2 0.0 copy-start.11
  7.2 0.0 all-gather.3.cloned.1.call-start
  7.2 1.3 copy-done
  8.6 1.8 fusion.20
  10.4 0.0 copy-done.11
  10.4 2.6 convolution_bitcast_fusion
  13.0 0.0 copy-start.10
  13.0 0.0 copy-start.16
  13.1 0.0 copy-start.13
  13.1 1.6 copy.23
  14.7 0.0 all-gather.3.cloned.1.call-update
  14.7 0.0 all-reduce.4.cloned.1.call-start
  14.8 0.0 copy-done.10
  14.8 0.0 copy-done.16
  14.8 1.6 convolution_bitcast_fusion.3
  16.4 129.7 %all-gather.3.cloned.1.call-done = f32[48,128,1024]{2,1,0:T(8,128)} async-done(((f32[3,128,1024]{2,1,0:T(8,128)}), f32[48,128,1024]{2,1,0:T(8,128)}) %all-gather.3.cloned.1.call-update) | async-done | bytes 25165840 | tf_op jit(solution)/shard_map/all_gather | solution.py:34
  146.1 9.3 %reduce_sum.27 = f32[3,128,1024]{2,1,0:T(8,128)S(1)} reduce(f32[16,3,128,1024]{3,2,1,0:T(8,128)} %bitcast.97, f32[]{:T(128)} %constant.12.clone.1), dimensions={0}, to_apply=%region_0.0 | reduce | flops 5898240 | bytes 26738692 | tf_op jit(solution)/shard_map/reduce_sum | solution.py:34
  155.5 0.0 copy-start.17
  155.5 1.0 fusion.53
  156.5 0.0 copy-start.7
  156.5 0.0 copy-start.9
  156.5 1.3 copy-done.7
  157.8 1.3 fusion.27
  159.1 0.0 copy-done.9
  159.1 0.0 copy-start.12
  159.1 0.0 copy-start.14
  159.1 0.0 copy-start.15
  159.2 1.1 pad_maximum_fusion
  160.2 0.0 all-reduce.4.cloned.1.call-update
  160.2 0.2 all-reduce.6.cloned.1.call-start
  160.5 0.1 select_reduce_fusion.1
  160.6 2.4 fusion.49
  162.9 91.2 %all-reduce.4.cloned.1.call-done = f32[2,128,1024]{2,1,0:T(8,128)} async-done(((f32[2,128,1024]{2,1,0:T(8,128)}), f32[2,128,1024]{2,1,0:T(8,128)}) %all-reduce.4.cloned.1.call-update) | async-done | bytes 1048592 | tf_op jit(solution)/shard_map/psum | solution.py:60
  254.1 1.6 fusion.37
  255.7 4.7 multiply_multiply_fusion.2
  260.5 0.0 copy-start.6
  260.5 1.1 fusion.21
  261.6 1.0 convolution_bitcast_fusion.2
  262.5 0.0 copy-done.1
  262.5 0.0 copy-done.6
  262.6 1.1 pad_maximum_fusion.1
  263.6 0.0 all-reduce.6.cloned.1.call-update
  263.7 0.0 all-reduce.8.cloned.1.call-start
  263.7 2.4 fusion.45
  266.1 90.6 %all-reduce.6.cloned.1.call-done = f32[2,128,1024]{2,1,0:T(8,128)} async-done(((f32[2,128,1024]{2,1,0:T(8,128)}), f32[2,128,1024]{2,1,0:T(8,128)}) %all-reduce.6.cloned.1.call-update) | async-done | bytes 1048592 | tf_op jit(solution)/shard_map/psum | solution.py:60
  356.7 1.6 fusion.39
  358.3 4.2 multiply_multiply_fusion.1
  362.5 0.0 copy-start.4
  362.5 0.0 copy-start.5
  362.5 1.0 convolution_bitcast_fusion.1
  363.5 2.1 copy-done.2
  365.6 1.3 fusion.24
  367.0 1.1 pad_maximum_fusion.2
  368.1 0.0 all-reduce.8.cloned.1.call-update
  368.1 0.9 constant_dynamic-slice_fusion.2
  369.0 0.1 copy.25
  369.1 91.9 %all-reduce.8.cloned.1.call-done = f32[2,128,1024]{2,1,0:T(8,128)} async-done(((f32[2,128,1024]{2,1,0:T(8,128)}), f32[2,128,1024]{2,1,0:T(8,128)}) %all-reduce.8.cloned.1.call-update) | async-done | bytes 1048592 | tf_op jit(solution)/shard_map/psum | solution.py:60
  461.0 1.6 fusion.41
  462.6 0.1 constant_dynamic-slice_fusion
  462.7 6.3 %multiply_multiply_fusion = (f32[512,1024]{1,0:T(8,128)}, f32[512,1024]{1,0:T(8,128)}) fusion(f32[512,1024]{1,0:T(8,128)} %copy-done.5, f32[512]{0:T(512)S(1)} %get-tuple-element.12, f32[512]{0:T(512)S(1)} %get-tuple-element.4, f32[512,1024]{1,0:T(8,128)} %fusion.45, bf16[512,3,1024]{2,0,1:T(8,128)(2,1)} %param.23, f32[512]{0:T(512)S(1)} %get-tuple-element.3, ...), kind=kOutput, calls=%fused_computation.15 | convolution fusion | flops 815333376 | bytes 14163968 | tf_op jit(solution)/shard_map/dot_general | solution.py:64
  469.1 0.1 copy.26
  469.2 0.1 copy.27
  469.2 0.7 pad_maximum_fusion.3
  (14 shorter events, 0.0 us)
Async XLA Ops:
  7.2 1.4 copy-start
  7.2 3.2 copy-start.11
  7.2 138.9 %all-gather.3.cloned.1.call-start = ((), (), s32[]{:S(2)}) async-start(), calls=%async_computation.3 | async-start | bytes 26738688 | tf_op jit(solution)/shard_map/all_gather | solution.py:34
  13.0 1.7 copy-start.10
  13.0 1.7 copy-start.16
  13.1 3.3 copy-start.13
  14.7 239.4 %all-reduce.4.cloned.1.call-start = ((), (), s32[]{:S(2)}) async-start(), calls=%async_computation | async-start | bytes 2097152 | tf_op jit(solution)/shard_map/psum | solution.py:60
  155.5 2.4 copy-start.17
  156.5 1.3 copy-start.7
  156.5 2.6 copy-start.9
  159.1 1.4 copy-start.12
  159.1 1.4 copy-start.14
  159.1 1.4 copy-start.15
  160.2 196.5 %all-reduce.6.cloned.1.call-start = ((), (), s32[]{:S(2)}) async-start(), calls=%async_computation.1 | async-start | bytes 2097152 | tf_op jit(solution)/shard_map/psum | solution.py:60
  255.7 4.8 copy-start.8
  260.5 2.1 copy-start.1
  260.5 2.1 copy-start.6
  263.7 197.4 %all-reduce.8.cloned.1.call-start = ((), (), s32[]{:S(2)}) async-start(), calls=%async_computation.2 | async-start | bytes 2097152 | tf_op jit(solution)/shard_map/psum | solution.py:60
  358.3 5.2 %copy-start.3 = (f32[512,1024]{1,0:T(8,128)S(1)}, f32[512,1024]{1,0:T(8,128)}, u32[]{:S(2)}) copy-start(f32[512,1024]{1,0:T(8,128)} %fusion.45) | copy-start | bytes 6291460
  362.5 4.5 copy-start.4
  362.5 4.5 copy-start.5
  362.5 3.1 copy-start.2
Sparse Core Ops, SparseCore 0:
  14.8 131.2 all-gather.2
  160.4 93.7 all-reduce.3
  263.8 92.8 all-reduce.5
  368.2 92.7 all-reduce.7
